TPU v7x, 128 devices: a whole 4x4x4 slice. The times are simulated.
128 devices in a mesh: mode: 8 (over z, y_hi), slab: 16 (over x, y_lo, core).
Axes of the slice: x: 4, y: 4 (y_hi: 2, y_lo: 2; y = y_hi * 2 + y_lo), z: 4, core: 2. Of those that a mesh axis runs over, the one named last changes fastest.
Arguments:
- modes: bfloat16 [48, 3, 32, 256, 128], P('mode', None, 'slab'), may hold values from -100 to 100
- volume: float32 [32, 256, 128], P(None, ('mode', 'slab')), may hold values from 0.5 to 24
Outputs:
- convective: float32 [2304, 48], P(('mode', 'slab'))
- dissipation: float32 [48, 48], replicated
All inputs are finite; a program needn't handle non-finite values.
Results may differ from a plain program's by a relative error of at most 0.0043.
Values may be sent and summed in bfloat16 or wider, within the bound.
A program may use at most 128 MiB of HBM per device.

v0:
```python
import math
import jax
import jax.numpy as jnp
from jax import lax
from jax.sharding import PartitionSpec as P

viscosity = 0.05


def extended(block, sides, width):
    for axis, dim in sides:
        count = lax.axis_size(axis)
        forward = [(i, i + 1) for i in range(count - 1)]
        backward = [(target, source) for source, target in forward]
        low = lax.ppermute(
            lax.slice_in_dim(block, block.shape[dim] - width, None, axis=dim), axis, forward
        )
        high = lax.ppermute(lax.slice_in_dim(block, 0, width, axis=dim), axis, backward)
        block = jnp.concatenate([low, block, high], axis=dim)
    return block


def stencil(padded, dim, length):
    shifted = [
        lax.slice_in_dim(padded, offset, offset + length, axis=dim).astype(jnp.float32)
        for offset in range(5)
    ]
    return (shifted[0] - 8.0 * shifted[1] + 8.0 * shifted[3] - shifted[4]) / 12.0


def gradient_fields(centre, x_padded, y_padded):
    z_padded = jnp.concatenate([centre[..., -2:], centre, centre[..., :2]], axis=4)
    along_x = stencil(x_padded, 2, centre.shape[2])
    along_y = stencil(y_padded, 3, centre.shape[3])
    along_z = stencil(z_padded, 4, centre.shape[4])
    return jnp.stack([along_x, along_y, along_z], axis=2).astype(jnp.bfloat16)


def regroup(stacked):
    return lax.all_to_all(
        lax.all_to_all(stacked, "mode", split_axis=3, concat_axis=0, tiled=True),
        "slab",
        split_axis=3,
        concat_axis=2,
        tiled=True,
    )


def contract(values, grad_all, weights, limit):
    mode_count = values.shape[0]
    cell_count = weights.size
    block_size = math.gcd(cell_count, limit)
    flat_values = values.reshape(mode_count, 3, cell_count)
    flat_grads = grad_all.reshape(mode_count, 3, 3, cell_count)
    flat_weights = weights.reshape(cell_count)

    def one_step(number, running):
        first_cell = number * block_size
        piece_values = lax.dynamic_slice_in_dim(flat_values, first_cell, block_size, 2)
        piece_grads = lax.dynamic_slice_in_dim(flat_grads, first_cell, block_size, 3)
        piece_weights = lax.dynamic_slice_in_dim(flat_weights, first_cell, block_size, 0)
        values_wide = piece_values.astype(jnp.float32)
        grads_wide = piece_grads.astype(jnp.float32)
        carried = values_wide[:, None, None, 0, :] * grads_wide[None, :, :, 0, :]
        carried = carried + values_wide[:, None, None, 1, :] * grads_wide[None, :, :, 1, :]
        carried = carried + values_wide[:, None, None, 2, :] * grads_wide[None, :, :, 2, :]
        carried = (
            (carried * piece_weights)
            .astype(jnp.bfloat16)
            .reshape(mode_count * mode_count, 3 * block_size)
        )
        conv_add = lax.dot_general(
            piece_values.reshape(mode_count, 3 * block_size),
            carried,
            (((1,), (1,)), ((), ())),
            preferred_element_type=jnp.float32,
        )
        weighted = (
            (grads_wide * piece_weights).astype(jnp.bfloat16).reshape(mode_count, 9 * block_size)
        )
        diss_add = lax.dot_general(
            piece_grads.reshape(mode_count, 9 * block_size),
            weighted,
            (((1,), (1,)), ((), ())),
            preferred_element_type=jnp.float32,
        )
        return (running[0] + conv_add, running[1] + diss_add)

    start_conv = jnp.zeros((mode_count, mode_count * mode_count), jnp.float32)
    start_diss = jnp.zeros((mode_count, mode_count), jnp.float32)
    conv_sum, diss_sum = lax.fori_loop(
        0, cell_count // block_size, one_step, (start_conv, start_diss)
    )
    return (conv_sum.reshape(mode_count * mode_count, mode_count), diss_sum)


def per_device(modes, volume):
    x_padded = extended(modes, (("slab", 2),), 2)
    y_padded = jnp.pad(modes, ((0, 0), (0, 0), (0, 0), (2, 2), (0, 0)))
    local_grads = gradient_fields(modes, x_padded, y_padded)
    local_count = modes.shape[0]
    stacked = jnp.concatenate(
        [modes, local_grads.reshape((local_count, 9) + modes.shape[2:])], axis=1
    )
    regrouped = regroup(stacked)
    values = regrouped[:, :3]
    grad_all = regrouped[:, 3:].reshape((regrouped.shape[0], 3, 3) + regrouped.shape[2:])
    conv_part, diss_part = contract(values, grad_all, volume, 1024)
    conv_sum = lax.psum_scatter(conv_part, ("mode", "slab"), scatter_dimension=0, tiled=True)
    diss_sum = lax.psum(diss_part, ("mode", "slab"))
    cell_total = (
        volume.shape[0]
        * volume.shape[1]
        * volume.shape[2]
        * lax.axis_size("mode")
        * lax.axis_size("slab")
    )
    convective = conv_sum * (1.0 / math.sqrt(cell_total))
    dissipation = diss_sum * (viscosity / cell_total)
    return (convective, dissipation)


def solution(mesh):
    placed = (P("mode", None, "slab", None, None), P(None, ("mode", "slab"), None))
    return jax.shard_map(
        per_device,
        mesh=mesh,
        in_specs=placed,
        out_specs=(P(("mode", "slab"), None), P()),
        check_vma=False,
    )
```

profile of v0, /device:TPU:1, one launch (start us, length us, event | category | flops | bytes accessed | tf_op | source)
XLA Modules:
  0.0 1076.9 jit_solution(17785046774700136053)
XLA Ops:
  7.2 3.4 collective-permute-start.1
  13.8 3.3 fusion.10
  17.1 21.5 %collective-permute-done.1 = bf16[6,3,2,256,128]{4,3,2,1,0:T(8,128)(2,1)S(1)} collective-permute-done((bf16[6,3,2,256,128]{4,3,2,1,0:T(8,128)(2,1)}, bf16[6,3,2,256,128]{4,3,2,1,0:T(8,128)(2,1)S(1)}, u32[]{:S(2)}, u32[]{:S(2)}) %collective-permute-start.1) | collective-permute-done | bytes 2359328 | tf_op jit(solution)/shard_map/ppermute | solution.py:18
  38.6 25.6 %collective-permute-done = bf16[6,3,2,256,128]{4,3,2,1,0:T(8,128)(2,1)S(1)} collective-permute-done((bf16[6,3,2,256,128]{4,3,2,1,0:T(8,128)(2,1)}, bf16[6,3,2,256,128]{4,3,2,1,0:T(8,128)(2,1)S(1)}, u32[]{:S(2)}, u32[]{:S(2)}) %collective-permute-start) | collective-permute-done | bytes 2359328 | tf_op jit(solution)/shard_map/ppermute | solution.py:15
  64.2 10.0 fusion.4
  74.2 3.5 pad_maximum_fusion.1
  77.7 7.5 pad_maximum_fusion
  85.1 17.6 %copy.54 = bf16[6,12,2,256,128]{4,2,1,0,3:T(2,128)(2,1)S(1)} copy(bf16[6,12,2,256,128]{4,3,2,1,0:T(8,128)(2,1)} %pad_maximum_fusion) | data formatting | bytes 18874368 | tf_op jit(solution)/shard_map/concatenate | solution.py:102
  102.7 69.1 %all_to_all.36 = bf16[6,12,2,256,128]{4,2,1,0,3:T(2,128)(2,1)} all-to-all(bf16[6,12,2,256,128]{4,2,1,0,3:T(2,128)(2,1)S(1)} %copy.54), channel_id=1, replica_groups=mesh['mode'=8,'slab'=16] {'mode'}, dimensions={3} | all-to-all | bytes 18874368 | tf_op jit(solution)/shard_map/all_to_all | solution.py:41
  171.8 9.8 copy.55
  181.6 10.4 copy.56
  192.1 14.8 %copy.57 = bf16[48,12,2,32,128]{4,2,1,0,3:T(2,128)(2,1)} copy(bf16[48,12,2,32,128]{4,3,2,1,0:T(8,128)(2,1)} %bitcast.74) | data formatting | bytes 18874368 | tf_op jit(solution)/shard_map/all_to_all | solution.py:41
  206.9 29.7 %all-to-all-start.1 = ((bf16[48,12,2,32,128]{4,2,1,0,3:T(2,128)(2,1)}), bf16[48,12,2,32,128]{4,2,1,0,3:T(2,128)(2,1)}, u32[]{:S(2)}, u32[]{:S(2)}) async-start(bf16[48,12,2,32,128]{4,2,1,0,3:T(2,128)(2,1)} %copy.57), calls=%async_computation.1 | async-start | bytes 18874368 | tf_op jit(solution)/shard_map/all_to_all | solution.py:40
  236.8 143.3 %all-to-all-done.1 = bf16[48,12,2,32,128]{4,2,1,0,3:T(2,128)(2,1)} async-done(((bf16[48,12,2,32,128]{4,2,1,0,3:T(2,128)(2,1)}), bf16[48,12,2,32,128]{4,2,1,0,3:T(2,128)(2,1)}, u32[]{:S(2)}, u32[]{:S(2)}) %all-to-all-start.1) | async-done | bytes 9437216 | tf_op jit(solution)/shard_map/all_to_all | solution.py:40
  380.1 9.4 copy.58
  389.5 10.3 copy.59
  401.9 4.8 slice.121
  406.7 8.9 copy.61
  415.6 16.2 %reshape_reshape.3 = bf16[48,3,3,8192]{3,0,2,1:T(8,128)(2,1)} reshape(bf16[48,9,32,2,128]{4,3,2,0,1:T(2,128)(2,1)} %copy.61) | data formatting | bytes 14155776 | tf_op jit(solution)/shard_map/reshape;reshape | solution.py:54
  431.8 4.1 copy.64
  435.9 6.1 reshape.98
  442.0 407.7 %while.16 = (s32[]{:T(128)}, f32[48,2304]{1,0:T(8,128)}, f32[48,48]{1,0:T(8,128)S(1)}, bf16[48,3,8192]{2,1,0:T(4,128)(2,1)}, bf16[48,3,3,8192]{3,0,2,1:T(8,128)(...) while((s32[]{:T(128)}, f32[48,2304]{1,0:T(8,128)}, ...), condition=%wide.region_1.2_spmd.clone, body=%wide.region_0.1_spmd.clone.sunk | while | flops 773485056 | bytes 75239088 | solution.py:91
  452.5 19.9 %multiply_convert_fusion.9 = bf16[48,48,3,1024]{3,2,1,0:T(4,128)(2,1)S(1)} fusion(f32[1024]{0:T(1024)S(1)} %dynamic_slice.40, f32[48,3,1024]{2,1,0:T(4,128)} %copy.84, f32[48,1024]{1,0:T(8,128)} %get-tuple-element.238, f32[48,3,1024]{2,1,0:T(4,128)} %copy.85, f32[48,1024]{1,0:T(8,128)} %get-tuple-element.240, f32[48,3,1024]{2,1,0:T(4,128)} %copy.86, ...), kind=kLoop, calls=%fused_computation.clone.1 | loop fusion | flops 49545216 | bytes 16519168 | tf_op jit(solution)/shard_map/while/body/eval_jaxpr/convert_element_type | solution.py:69
  472.4 10.4 copy.88
  482.8 10.1 convolution_add_fusion.2
  503.5 19.9 %multiply_convert_fusion.9 = bf16[48,48,3,1024]{3,2,1,0:T(4,128)(2,1)S(1)} fusion(f32[1024]{0:T(1024)S(1)} %dynamic_slice.40, f32[48,3,1024]{2,1,0:T(4,128)} %copy.84, f32[48,1024]{1,0:T(8,128)} %get-tuple-element.238, f32[48,3,1024]{2,1,0:T(4,128)} %copy.85, f32[48,1024]{1,0:T(8,128)} %get-tuple-element.240, f32[48,3,1024]{2,1,0:T(4,128)} %copy.86, ...), kind=kLoop, calls=%fused_computation.clone.1 | loop fusion | flops 49545216 | bytes 16519168 | tf_op jit(solution)/shard_map/while/body/eval_jaxpr/convert_element_type | solution.py:69
  523.4 10.4 copy.88
  533.7 10.1 convolution_add_fusion.2
  554.4 19.9 %multiply_convert_fusion.9 = bf16[48,48,3,1024]{3,2,1,0:T(4,128)(2,1)S(1)} fusion(f32[1024]{0:T(1024)S(1)} %dynamic_slice.40, f32[48,3,1024]{2,1,0:T(4,128)} %copy.84, f32[48,1024]{1,0:T(8,128)} %get-tuple-element.238, f32[48,3,1024]{2,1,0:T(4,128)} %copy.85, f32[48,1024]{1,0:T(8,128)} %get-tuple-element.240, f32[48,3,1024]{2,1,0:T(4,128)} %copy.86, ...), kind=kLoop, calls=%fused_computation.clone.1 | loop fusion | flops 49545216 | bytes 16519168 | tf_op jit(solution)/shard_map/while/body/eval_jaxpr/convert_element_type | solution.py:69
  574.3 10.4 copy.88
  584.7 10.1 convolution_add_fusion.2
  605.4 19.9 %multiply_convert_fusion.9 = bf16[48,48,3,1024]{3,2,1,0:T(4,128)(2,1)S(1)} fusion(f32[1024]{0:T(1024)S(1)} %dynamic_slice.40, f32[48,3,1024]{2,1,0:T(4,128)} %copy.84, f32[48,1024]{1,0:T(8,128)} %get-tuple-element.238, f32[48,3,1024]{2,1,0:T(4,128)} %copy.85, f32[48,1024]{1,0:T(8,128)} %get-tuple-element.240, f32[48,3,1024]{2,1,0:T(4,128)} %copy.86, ...), kind=kLoop, calls=%fused_computation.clone.1 | loop fusion | flops 49545216 | bytes 16519168 | tf_op jit(solution)/shard_map/while/body/eval_jaxpr/convert_element_type | solution.py:69
  625.3 10.4 copy.88
  635.6 10.1 convolution_add_fusion.2
  656.4 19.9 %multiply_convert_fusion.9 = bf16[48,48,3,1024]{3,2,1,0:T(4,128)(2,1)S(1)} fusion(f32[1024]{0:T(1024)S(1)} %dynamic_slice.40, f32[48,3,1024]{2,1,0:T(4,128)} %copy.84, f32[48,1024]{1,0:T(8,128)} %get-tuple-element.238, f32[48,3,1024]{2,1,0:T(4,128)} %copy.85, f32[48,1024]{1,0:T(8,128)} %get-tuple-element.240, f32[48,3,1024]{2,1,0:T(4,128)} %copy.86, ...), kind=kLoop, calls=%fused_computation.clone.1 | loop fusion | flops 49545216 | bytes 16519168 | tf_op jit(solution)/shard_map/while/body/eval_jaxpr/convert_element_type | solution.py:69
  676.3 10.4 copy.88
  686.7 10.1 convolution_add_fusion.2
  707.4 19.9 %multiply_convert_fusion.9 = bf16[48,48,3,1024]{3,2,1,0:T(4,128)(2,1)S(1)} fusion(f32[1024]{0:T(1024)S(1)} %dynamic_slice.40, f32[48,3,1024]{2,1,0:T(4,128)} %copy.84, f32[48,1024]{1,0:T(8,128)} %get-tuple-element.238, f32[48,3,1024]{2,1,0:T(4,128)} %copy.85, f32[48,1024]{1,0:T(8,128)} %get-tuple-element.240, f32[48,3,1024]{2,1,0:T(4,128)} %copy.86, ...), kind=kLoop, calls=%fused_computation.clone.1 | loop fusion | flops 49545216 | bytes 16519168 | tf_op jit(solution)/shard_map/while/body/eval_jaxpr/convert_element_type | solution.py:69
  727.3 10.4 copy.88
  737.7 10.1 convolution_add_fusion.2
  758.3 19.9 %multiply_convert_fusion.9 = bf16[48,48,3,1024]{3,2,1,0:T(4,128)(2,1)S(1)} fusion(f32[1024]{0:T(1024)S(1)} %dynamic_slice.40, f32[48,3,1024]{2,1,0:T(4,128)} %copy.84, f32[48,1024]{1,0:T(8,128)} %get-tuple-element.238, f32[48,3,1024]{2,1,0:T(4,128)} %copy.85, f32[48,1024]{1,0:T(8,128)} %get-tuple-element.240, f32[48,3,1024]{2,1,0:T(4,128)} %copy.86, ...), kind=kLoop, calls=%fused_computation.clone.1 | loop fusion | flops 49545216 | bytes 16519168 | tf_op jit(solution)/shard_map/while/body/eval_jaxpr/convert_element_type | solution.py:69
  778.2 10.4 copy.88
  788.6 10.1 convolution_add_fusion.2
  809.3 19.9 %multiply_convert_fusion.9 = bf16[48,48,3,1024]{3,2,1,0:T(4,128)(2,1)S(1)} fusion(f32[1024]{0:T(1024)S(1)} %dynamic_slice.40, f32[48,3,1024]{2,1,0:T(4,128)} %copy.84, f32[48,1024]{1,0:T(8,128)} %get-tuple-element.238, f32[48,3,1024]{2,1,0:T(4,128)} %copy.85, f32[48,1024]{1,0:T(8,128)} %get-tuple-element.240, f32[48,3,1024]{2,1,0:T(4,128)} %copy.86, ...), kind=kLoop, calls=%fused_computation.clone.1 | loop fusion | flops 49545216 | bytes 16519168 | tf_op jit(solution)/shard_map/while/body/eval_jaxpr/convert_element_type | solution.py:69
  829.2 10.4 copy.88
  839.6 10.1 convolution_add_fusion.2
  849.7 70.5 %psum.7 = f32[48,48]{1,0:T(8,128)S(1)} all-reduce(f32[48,48]{1,0:T(8,128)S(1)} %get-tuple-element.113), channel_id=1, replica_groups=mesh['mode'=8,'slab'=16] {'mode','slab'}, use_global_device_ids=true, to_apply=%region_3.4 | all-reduce | flops 2304 | bytes 18432 | tf_op jit(solution)/shard_map/psum | solution.py:110
  923.7 145.1 %all-reduce.4.cloned.1.call-done = f32[2304,48]{1,0:T(8,128)} async-done(((f32[2304,48]{1,0:T(8,128)}), f32[2304,48]{1,0:T(8,128)}) %all-reduce.4.cloned.1.call-update) | async-done | bytes 442384
  (107 shorter events, 94.6 us)
Async XLA Ops:
  7.2 57.0 %copy-start = (bf16[6,3,2,256,128]{4,3,2,1,0:T(8,128)(2,1)S(1)}, bf16[6,3,2,256,128]{4,3,2,1,0:T(8,128)(2,1)}, u32[]{:S(2)}) copy-start(bf16[6,3,2,256,128]{4,3,2,1,0:T(8,128)(2,1)} %param.4) | copy-start | bytes 7077892
  7.2 31.4 %collective-permute-start.1 = (bf16[6,3,2,256,128]{4,3,2,1,0:T(8,128)(2,1)}, bf16[6,3,2,256,128]{4,3,2,1,0:T(8,128)(2,1)S(1)}, u32[]{:S(2)}, u32[]{:S(2)}) collective-permute-start(bf16[6,3,2,256,128]{4,3,2,1,0:T(8,128)(2,1)} %param.4), channel_id=1, source_target_pairs={{1,0},{2,1},{3,2},{4,3},{5,4},{6,5},{7,6},{8,7},{9,8},{10,9},{11,1... | collective-permute-start | bytes 7077896 | tf_op jit(solution)/shard_map/ppermute | solution.py:18
  10.6 53.6 %collective-permute-start = (bf16[6,3,2,256,128]{4,3,2,1,0:T(8,128)(2,1)}, bf16[6,3,2,256,128]{4,3,2,1,0:T(8,128)(2,1)S(1)}, u32[]{:S(2)}, u32[]{:S(2)}) collective-permute-start(bf16[6,3,2,256,128]{4,3,2,1,0:T(8,128)(2,1)} %param.4), channel_id=1, source_target_pairs={{0,1},{1,2},{2,3},{3,4},{4,5},{5,6},{6,7},{7,8},{8,9},{9,10},{10,1... | collective-permute-start | bytes 7077896 | tf_op jit(solution)/shard_map/ppermute | solution.py:15
  206.9 173.2 %all-to-all-start.1 = ((bf16[48,12,2,32,128]{4,2,1,0,3:T(2,128)(2,1)}), bf16[48,12,2,32,128]{4,2,1,0,3:T(2,128)(2,1)}, u32[]{:S(2)}, u32[]{:S(2)}) async-start(bf16[48,12,2,32,128]{4,2,1,0,3:T(2,128)(2,1)} %copy.57), calls=%async_computation.1 | async-start | bytes 18874368 | tf_op jit(solution)/shard_map/all_to_all | solution.py:40
  236.5 832.2 %all-reduce.4.cloned.1.call-start = ((), (), s32[]{:S(2)}) async-start(), calls=%async_computation.2 | async-start | bytes 2359296
Sparse Core Ops, SparseCore 0:
  923.2 145.5 all-reduce.3
where the time goes:
time: 1080 us
  waiting for transfers between devices  335 us (31%)
  local copies, waits for them, and re-layouts  262 us (24%)
  other arithmetic  193 us (18%)
  blocking collectives  140 us (13%)
  matrix products  95.9 us (9%)
  starting transfers between devices  36.5 us (3%)
  between operations  14.1 us (1%)
    convert_element_type x8, other arithmetic, one_step(): carried = (carried * piece_weights).astype(jnp.bfloat16).reshape(mode_cou...  159 us
    unnamed x2, waiting for transfers between devices  145 us
    all_to_all x1, waiting for transfers between devices, regroup(): lax.all_to_all(lax.all_to_all(stacked, 'mode', split_axis=3, concat_axis=...  143 us
    while x32, local copies, waits for them, and re-layouts  90.8 us
    dot_general x8, matrix products, one_step(): lax.dot_general(piece_values.reshape(mode_count, 3 * block_size), carried...  81 us
    psum x1, blocking collectives, per_device(): diss_sum = lax.psum(diss_part, ('mode', 'slab'))  70.5 us
    all_to_all x1, blocking collectives, regroup(): lax.all_to_all(stacked, 'mode', split_axis=3, concat_axis=0, tiled=True)  69.1 us
    all_to_all x3, local copies, waits for them, and re-layouts, regroup(): lax.all_to_all(stacked, 'mode', split_axis=3, concat_axis=0, tiled=True)  35.1 us
  transfers between devices with their start and end apart: 4, of which 4 were waited for; matrix products, arithmetic and copies ran while one was open for 0% of the time, Pallas kernels for 0%

commit v1 on v0

--- a/solution.py
+++ b/solution.py
@@ -107,7 +107,8 @@
     grad_all = regrouped[:, 3:].reshape((regrouped.shape[0], 3, 3) + regrouped.shape[2:])
     conv_part, diss_part = contract(values, grad_all, volume, 1024)
     conv_sum = lax.psum_scatter(conv_part, ("mode", "slab"), scatter_dimension=0, tiled=True)
-    diss_sum = lax.psum(diss_part, ("mode", "slab"))
+    parts = lax.all_gather(diss_part, ("mode", "slab"))
+    diss_sum = jnp.sum(parts, axis=0)
     cell_total = (
         volume.shape[0]
         * volume.shape[1]

time: 1080 us -> 1210 us (1.12)
  waiting for transfers between devices: 335 us -> 539 us
  blocking collectives: 140 us -> 69.1 us
    all_gather x0 -> x1, waiting for transfers between devices: none -> 196 us  [per_device(): parts = lax.all_gather(diss_part, ('mode', 'slab'))]
    psum x1 -> x0, blocking collectives: 70.5 us -> none  [per_device(): diss_sum = lax.psum(diss_part, ('mode', 'slab'))]
    unnamed x2 -> x3, waiting for transfers between devices: 145 us -> 153 us
  transfers between devices with their start and end apart: 4 -> 5, of which waited for: 4 -> 5; matrix products, arithmetic and copies ran while one was open for 0% -> 0% of each run, Pallas kernels for 0% -> 0%
where the time goes in v1:
time: 1210 us
  waiting for transfers between devices  539 us (45%)
  local copies, waits for them, and re-layouts  261 us (22%)
  other arithmetic  195 us (16%)
  matrix products  95.8 us (8%)
  blocking collectives  69.1 us (6%)
  starting transfers between devices  36.5 us (3%)
  between operations  14.1 us (1%)
    all_gather x1, waiting for transfers between devices, per_device(): parts = lax.all_gather(diss_part, ('mode', 'slab'))  196 us
    convert_element_type x8, other arithmetic, one_step(): carried = (carried * piece_weights).astype(jnp.bfloat16).reshape(mode_cou...  159 us
    unnamed x3, waiting for transfers between devices  153 us
    all_to_all x1, waiting for transfers between devices, regroup(): lax.all_to_all(lax.all_to_all(stacked, 'mode', split_axis=3, concat_axis=...  143 us
    while x32, local copies, waits for them, and re-layouts  89.9 us
    dot_general x8, matrix products, one_step(): lax.dot_general(piece_values.reshape(mode_count, 3 * block_size), carried...  80.9 us
    all_to_all x1, blocking collectives, regroup(): lax.all_to_all(stacked, 'mode', split_axis=3, concat_axis=0, tiled=True)  69.1 us
    all_to_all x3, local copies, waits for them, and re-layouts, regroup(): lax.all_to_all(stacked, 'mode', split_axis=3, concat_axis=0, tiled=True)  35.1 us
  transfers between devices with their start and end apart: 5, of which 5 were waited for; matrix products, arithmetic and copies ran while one was open for 0% of the time, Pallas kernels for 0%

profile of v1, /device:TPU:1, one launch (start us, length us, event | category | flops | bytes accessed | tf_op | source)
XLA Modules:
  0.0 1211.6 jit_solution(5641633230011245620)
XLA Ops:
  7.2 3.4 collective-permute-start.1
  13.8 3.3 fusion.10
  17.1 21.5 %collective-permute-done.1 = bf16[6,3,2,256,128]{4,3,2,1,0:T(8,128)(2,1)S(1)} collective-permute-done((bf16[6,3,2,256,128]{4,3,2,1,0:T(8,128)(2,1)}, bf16[6,3,2,256,128]{4,3,2,1,0:T(8,128)(2,1)S(1)}, u32[]{:S(2)}, u32[]{:S(2)}) %collective-permute-start.1) | collective-permute-done | bytes 2359328 | tf_op jit(solution)/shard_map/ppermute | solution.py:18
  38.6 25.6 %collective-permute-done = bf16[6,3,2,256,128]{4,3,2,1,0:T(8,128)(2,1)S(1)} collective-permute-done((bf16[6,3,2,256,128]{4,3,2,1,0:T(8,128)(2,1)}, bf16[6,3,2,256,128]{4,3,2,1,0:T(8,128)(2,1)S(1)}, u32[]{:S(2)}, u32[]{:S(2)}) %collective-permute-start) | collective-permute-done | bytes 2359328 | tf_op jit(solution)/shard_map/ppermute | solution.py:15
  64.2 10.0 fusion.4
  74.2 3.5 pad_maximum_fusion.1
  77.6 7.5 pad_maximum_fusion
  85.1 17.6 %copy.54 = bf16[6,12,2,256,128]{4,2,1,0,3:T(2,128)(2,1)S(1)} copy(bf16[6,12,2,256,128]{4,3,2,1,0:T(8,128)(2,1)} %pad_maximum_fusion) | data formatting | bytes 18874368 | tf_op jit(solution)/shard_map/concatenate | solution.py:102
  102.7 69.1 %all_to_all.36 = bf16[6,12,2,256,128]{4,2,1,0,3:T(2,128)(2,1)} all-to-all(bf16[6,12,2,256,128]{4,2,1,0,3:T(2,128)(2,1)S(1)} %copy.54), channel_id=1, replica_groups=mesh['mode'=8,'slab'=16] {'mode'}, dimensions={3} | all-to-all | bytes 18874368 | tf_op jit(solution)/shard_map/all_to_all | solution.py:41
  171.8 9.8 copy.55
  181.7 10.4 copy.56
  192.1 14.8 %copy.57 = bf16[48,12,2,32,128]{4,2,1,0,3:T(2,128)(2,1)} copy(bf16[48,12,2,32,128]{4,3,2,1,0:T(8,128)(2,1)} %bitcast.75) | data formatting | bytes 18874368 | tf_op jit(solution)/shard_map/all_to_all | solution.py:41
  206.9 29.6 %all-to-all-start.1 = ((bf16[48,12,2,32,128]{4,2,1,0,3:T(2,128)(2,1)}), bf16[48,12,2,32,128]{4,2,1,0,3:T(2,128)(2,1)}, u32[]{:S(2)}, u32[]{:S(2)}) async-start(bf16[48,12,2,32,128]{4,2,1,0,3:T(2,128)(2,1)} %copy.57), calls=%async_computation.1 | async-start | bytes 18874368 | tf_op jit(solution)/shard_map/all_to_all | solution.py:40
  236.8 143.2 %all-to-all-done.1 = bf16[48,12,2,32,128]{4,2,1,0,3:T(2,128)(2,1)} async-done(((bf16[48,12,2,32,128]{4,2,1,0,3:T(2,128)(2,1)}), bf16[48,12,2,32,128]{4,2,1,0,3:T(2,128)(2,1)}, u32[]{:S(2)}, u32[]{:S(2)}) %all-to-all-start.1) | async-done | bytes 9437216 | tf_op jit(solution)/shard_map/all_to_all | solution.py:40
  380.0 9.4 copy.58
  389.4 10.3 copy.59
  401.8 4.8 slice.121
  406.6 9.0 copy.61
  415.6 16.2 %reshape_reshape.3 = bf16[48,3,3,8192]{3,0,2,1:T(8,128)(2,1)} reshape(bf16[48,9,32,2,128]{4,3,2,0,1:T(2,128)(2,1)} %copy.61) | data formatting | bytes 14155776 | tf_op jit(solution)/shard_map/reshape;reshape | solution.py:54
  431.7 4.1 copy.64
  435.8 6.1 reshape.99
  441.9 406.8 %while.16 = (s32[]{:T(128)}, f32[48,2304]{1,0:T(8,128)}, f32[48,48]{1,0:T(8,128)S(1)}, bf16[48,3,8192]{2,1,0:T(4,128)(2,1)}, bf16[48,3,3,8192]{3,0,2,1:T(8,128)(...) while((s32[]{:T(128)}, f32[48,2304]{1,0:T(8,128)}, ...), condition=%wide.region_1.2_spmd.clone, body=%wide.region_0.1_spmd.clone.sunk | while | flops 773485056 | bytes 75239088 | solution.py:91
  452.6 19.9 %multiply_convert_fusion.9 = bf16[48,48,3,1024]{3,2,1,0:T(4,128)(2,1)S(1)} fusion(f32[1024]{0:T(1024)S(1)} %dynamic_slice.40, f32[48,3,1024]{2,1,0:T(4,128)} %copy.84, f32[48,1024]{1,0:T(8,128)} %get-tuple-element.238, f32[48,3,1024]{2,1,0:T(4,128)} %copy.85, f32[48,1024]{1,0:T(8,128)} %get-tuple-element.240, f32[48,3,1024]{2,1,0:T(4,128)} %copy.86, ...), kind=kLoop, calls=%fused_computation.clone.1 | loop fusion | flops 49545216 | bytes 16519168 | tf_op jit(solution)/shard_map/while/body/eval_jaxpr/convert_element_type | solution.py:69
  472.5 10.3 copy.88
  482.7 10.1 convolution_add_fusion.2
  503.4 19.9 %multiply_convert_fusion.9 = bf16[48,48,3,1024]{3,2,1,0:T(4,128)(2,1)S(1)} fusion(f32[1024]{0:T(1024)S(1)} %dynamic_slice.40, f32[48,3,1024]{2,1,0:T(4,128)} %copy.84, f32[48,1024]{1,0:T(8,128)} %get-tuple-element.238, f32[48,3,1024]{2,1,0:T(4,128)} %copy.85, f32[48,1024]{1,0:T(8,128)} %get-tuple-element.240, f32[48,3,1024]{2,1,0:T(4,128)} %copy.86, ...), kind=kLoop, calls=%fused_computation.clone.1 | loop fusion | flops 49545216 | bytes 16519168 | tf_op jit(solution)/shard_map/while/body/eval_jaxpr/convert_element_type | solution.py:69
  523.3 10.3 copy.88
  533.6 10.1 convolution_add_fusion.2
  554.2 19.9 %multiply_convert_fusion.9 = bf16[48,48,3,1024]{3,2,1,0:T(4,128)(2,1)S(1)} fusion(f32[1024]{0:T(1024)S(1)} %dynamic_slice.40, f32[48,3,1024]{2,1,0:T(4,128)} %copy.84, f32[48,1024]{1,0:T(8,128)} %get-tuple-element.238, f32[48,3,1024]{2,1,0:T(4,128)} %copy.85, f32[48,1024]{1,0:T(8,128)} %get-tuple-element.240, f32[48,3,1024]{2,1,0:T(4,128)} %copy.86, ...), kind=kLoop, calls=%fused_computation.clone.1 | loop fusion | flops 49545216 | bytes 16519168 | tf_op jit(solution)/shard_map/while/body/eval_jaxpr/convert_element_type | solution.py:69
  574.1 10.3 copy.88
  584.4 10.1 convolution_add_fusion.2
  605.1 19.9 %multiply_convert_fusion.9 = bf16[48,48,3,1024]{3,2,1,0:T(4,128)(2,1)S(1)} fusion(f32[1024]{0:T(1024)S(1)} %dynamic_slice.40, f32[48,3,1024]{2,1,0:T(4,128)} %copy.84, f32[48,1024]{1,0:T(8,128)} %get-tuple-element.238, f32[48,3,1024]{2,1,0:T(4,128)} %copy.85, f32[48,1024]{1,0:T(8,128)} %get-tuple-element.240, f32[48,3,1024]{2,1,0:T(4,128)} %copy.86, ...), kind=kLoop, calls=%fused_computation.clone.1 | loop fusion | flops 49545216 | bytes 16519168 | tf_op jit(solution)/shard_map/while/body/eval_jaxpr/convert_element_type | solution.py:69
  625.0 10.3 copy.88
  635.2 10.1 convolution_add_fusion.2
  655.9 19.9 %multiply_convert_fusion.9 = bf16[48,48,3,1024]{3,2,1,0:T(4,128)(2,1)S(1)} fusion(f32[1024]{0:T(1024)S(1)} %dynamic_slice.40, f32[48,3,1024]{2,1,0:T(4,128)} %copy.84, f32[48,1024]{1,0:T(8,128)} %get-tuple-element.238, f32[48,3,1024]{2,1,0:T(4,128)} %copy.85, f32[48,1024]{1,0:T(8,128)} %get-tuple-element.240, f32[48,3,1024]{2,1,0:T(4,128)} %copy.86, ...), kind=kLoop, calls=%fused_computation.clone.1 | loop fusion | flops 49545216 | bytes 16519168 | tf_op jit(solution)/shard_map/while/body/eval_jaxpr/convert_element_type | solution.py:69
  675.8 10.3 copy.88
  686.1 10.1 convolution_add_fusion.2
  706.8 19.9 %multiply_convert_fusion.9 = bf16[48,48,3,1024]{3,2,1,0:T(4,128)(2,1)S(1)} fusion(f32[1024]{0:T(1024)S(1)} %dynamic_slice.40, f32[48,3,1024]{2,1,0:T(4,128)} %copy.84, f32[48,1024]{1,0:T(8,128)} %get-tuple-element.238, f32[48,3,1024]{2,1,0:T(4,128)} %copy.85, f32[48,1024]{1,0:T(8,128)} %get-tuple-element.240, f32[48,3,1024]{2,1,0:T(4,128)} %copy.86, ...), kind=kLoop, calls=%fused_computation.clone.1 | loop fusion | flops 49545216 | bytes 16519168 | tf_op jit(solution)/shard_map/while/body/eval_jaxpr/convert_element_type | solution.py:69
  726.7 10.3 copy.88
  736.9 10.1 convolution_add_fusion.2
  757.6 19.9 %multiply_convert_fusion.9 = bf16[48,48,3,1024]{3,2,1,0:T(4,128)(2,1)S(1)} fusion(f32[1024]{0:T(1024)S(1)} %dynamic_slice.40, f32[48,3,1024]{2,1,0:T(4,128)} %copy.84, f32[48,1024]{1,0:T(8,128)} %get-tuple-element.238, f32[48,3,1024]{2,1,0:T(4,128)} %copy.85, f32[48,1024]{1,0:T(8,128)} %get-tuple-element.240, f32[48,3,1024]{2,1,0:T(4,128)} %copy.86, ...), kind=kLoop, calls=%fused_computation.clone.1 | loop fusion | flops 49545216 | bytes 16519168 | tf_op jit(solution)/shard_map/while/body/eval_jaxpr/convert_element_type | solution.py:69
  777.5 10.3 copy.88
  787.8 10.1 convolution_add_fusion.2
  808.4 19.9 %multiply_convert_fusion.9 = bf16[48,48,3,1024]{3,2,1,0:T(4,128)(2,1)S(1)} fusion(f32[1024]{0:T(1024)S(1)} %dynamic_slice.40, f32[48,3,1024]{2,1,0:T(4,128)} %copy.84, f32[48,1024]{1,0:T(8,128)} %get-tuple-element.238, f32[48,3,1024]{2,1,0:T(4,128)} %copy.85, f32[48,1024]{1,0:T(8,128)} %get-tuple-element.240, f32[48,3,1024]{2,1,0:T(4,128)} %copy.86, ...), kind=kLoop, calls=%fused_computation.clone.1 | loop fusion | flops 49545216 | bytes 16519168 | tf_op jit(solution)/shard_map/while/body/eval_jaxpr/convert_element_type | solution.py:69
  828.3 10.3 copy.88
  838.6 10.1 convolution_add_fusion.2
  852.3 152.4 %all-reduce.4.cloned.1.call-done = f32[2304,48]{1,0:T(8,128)} async-done(((f32[2304,48]{1,0:T(8,128)}), f32[2304,48]{1,0:T(8,128)}) %all-reduce.4.cloned.1.call-update) | async-done | bytes 442384
  1006.1 195.9 %all-gather.3.cloned.1.call-done = f32[6144,48]{1,0:T(8,128)} async-done(((f32[48,48]{1,0:T(8,128)}), f32[6144,48]{1,0:T(8,128)}) %all-gather.3.cloned.1.call-update) | async-done | bytes 1179664 | tf_op jit(solution)/shard_map/all_gather | solution.py:110
  (112 shorter events, 97.4 us)
Async XLA Ops:
  7.2 57.0 %copy-start = (bf16[6,3,2,256,128]{4,3,2,1,0:T(8,128)(2,1)S(1)}, bf16[6,3,2,256,128]{4,3,2,1,0:T(8,128)(2,1)}, u32[]{:S(2)}) copy-start(bf16[6,3,2,256,128]{4,3,2,1,0:T(8,128)(2,1)} %param.4) | copy-start | bytes 7077892
  7.2 31.4 %collective-permute-start.1 = (bf16[6,3,2,256,128]{4,3,2,1,0:T(8,128)(2,1)}, bf16[6,3,2,256,128]{4,3,2,1,0:T(8,128)(2,1)S(1)}, u32[]{:S(2)}, u32[]{:S(2)}) collective-permute-start(bf16[6,3,2,256,128]{4,3,2,1,0:T(8,128)(2,1)} %param.4), channel_id=1, source_target_pairs={{1,0},{2,1},{3,2},{4,3},{5,4},{6,5},{7,6},{8,7},{9,8},{10,9},{11,1... | collective-permute-start | bytes 7077896 | tf_op jit(solution)/shard_map/ppermute | solution.py:18
  10.6 53.6 %collective-permute-start = (bf16[6,3,2,256,128]{4,3,2,1,0:T(8,128)(2,1)}, bf16[6,3,2,256,128]{4,3,2,1,0:T(8,128)(2,1)S(1)}, u32[]{:S(2)}, u32[]{:S(2)}) collective-permute-start(bf16[6,3,2,256,128]{4,3,2,1,0:T(8,128)(2,1)} %param.4), channel_id=1, source_target_pairs={{0,1},{1,2},{2,3},{3,4},{4,5},{5,6},{6,7},{7,8},{8,9},{9,10},{10,1... | collective-permute-start | bytes 7077896 | tf_op jit(solution)/shard_map/ppermute | solution.py:15
  206.9 173.1 %all-to-all-start.1 = ((bf16[48,12,2,32,128]{4,2,1,0,3:T(2,128)(2,1)}), bf16[48,12,2,32,128]{4,2,1,0,3:T(2,128)(2,1)}, u32[]{:S(2)}, u32[]{:S(2)}) async-start(bf16[48,12,2,32,128]{4,2,1,0,3:T(2,128)(2,1)} %copy.57), calls=%async_computation.1 | async-start | bytes 18874368 | tf_op jit(solution)/shard_map/all_to_all | solution.py:40
  236.5 768.2 %all-reduce.4.cloned.1.call-start = ((), (), s32[]{:S(2)}) async-start(), calls=%async_computation.3 | async-start | bytes 2359296
  848.7 2.9 copy-start.1
  851.5 350.4 %all-gather.3.cloned.1.call-start = ((), (), s32[]{:S(2)}) async-start(), calls=%async_computation.2 | async-start | bytes 3170304 | tf_op jit(solution)/shard_map/all_gather | solution.py:110
Sparse Core Ops, SparseCore 0:
  851.7 153.0 all-reduce.3
  1007.0 194.8 all-gather.2
